TPU v7x, 256 devices: a whole 4x4x8 slice. The times are simulated.
256 devices in a mesh: section: 4 (over x), expert: 32 (over z, y), mp: 2 (over core).
Axes of the slice: x: 4, y: 4, z: 8, core: 2. Of those that a mesh axis runs over, the one named last changes fastest.
Arguments:
- out_grad: bfloat16 [4, 4096, 4096], P('section', 'expert', 'mp'), may hold values from -6 to 6
- expert_ids: int32 [4, 4096, 2], P('section', 'expert'), may hold values from 0 to 31, all different within a row; in each aligned block of 128 rows (0 to 127, 128 to 255, ..., all dimensions but the last counted through in order) at most 16 rows name the same one
- gate_codes: int32 [4, 4096, 2], P('section', 'expert'), may hold values from 1 to 255
- up_weight: bfloat16 [4, 32, 4096, 1024], P('section', 'expert', None, 'mp'), may hold values from -0.09375 to 0.09375
- down_weight: bfloat16 [4, 32, 1024, 4096], P('section', 'expert', 'mp'), may hold values from -0.1875 to 0.1875
- pre_act: bfloat16 [4, 32, 512, 1024], P('section', 'expert', None, 'mp'), may hold values from -6 to 6
- conv_grad: bfloat16 [4, 4096, 4096], P('section', 'expert', 'mp'), may hold values from -6 to 6
- conv_input: bfloat16 [4, 4096, 4096], P('section', 'expert', 'mp'), may hold values from -0.09375 to 0.09375
- conv_weight: float32 [4, 4, 4096], P('section', None, 'mp'), may hold values from -3 to 3
- in_proj: bfloat16 [4, 4096, 4096], P('section', 'expert', 'mp'), may hold values from -0.09375 to 0.09375
Outputs:
- residual_to_previous: bfloat16 [4, 4096, 4096], P('section', 'expert', 'mp')
- kernel_grad: float32 [4, 4, 4096], P('section', None, 'mp')
Inputs may be any that keep to these rules, and one draw needn't show every extreme that they name: `expert_ids`: each token names two different experts; in every section, the tokens of one block of 128 name no expert more than 16 times, a bound that some block reaches.
All inputs are finite; a program needn't handle non-finite values.
Results may differ from a plain program's by a relative error of at most 0.0044.
Values may be sent and summed in bfloat16 or wider, within the bound.
A program may use at most 128 MiB of HBM per device.

v0:
```python
import jax
import jax.numpy as jnp
from jax import lax
from jax.sharding import PartitionSpec as P


def shifted(array, axis, by):
    size = lax.axis_size(axis)
    pairs = [(i, i + by) for i in range(size) if 0 <= i + by < size]
    return lax.ppermute(array, axis, pairs)


def silu_slope(pre_value):
    sig = jax.nn.sigmoid(pre_value)
    return sig * (1.0 + pre_value * (1.0 - sig))


def gated_rows(gates, rows, tok_rows):
    scaled = (gates[:, :, None] * rows.astype(jnp.float32)[:, None, :]).astype(jnp.bfloat16)
    return scaled.reshape(tok_rows * 2, rows.shape[1])


def fill_buffer(scaled, target, experts, capacity):
    width = scaled.shape[1]
    buffer = jnp.zeros((experts * capacity, width), jnp.bfloat16).at[target].set(scaled)
    return buffer.reshape(experts, capacity, width)


def shards(
    out_grad,
    expert_ids,
    gate_codes,
    up_weight,
    down_weight,
    pre_act,
    conv_grad,
    conv_input,
    conv_weight,
    in_proj,
):
    grad_rows = out_grad[0]
    route_ids = expert_ids[0]
    tok_rows = grad_rows.shape[0]
    experts = lax.axis_size("expert")
    capacity = pre_act.shape[2] // experts
    gates = gate_codes[0].astype(jnp.float32) / 256.0
    flat_ids = route_ids.reshape(tok_rows * 2)
    onehot = (flat_ids[:, None] == jnp.arange(experts, dtype=jnp.int32)[None, :]).astype(jnp.int32)
    before = jnp.cumsum(onehot, axis=0) - onehot
    position = jnp.sum(before * onehot, axis=1)
    target = flat_ids * capacity + position
    whole_rows = lax.all_gather(grad_rows, "mp", axis=1, tiled=True)
    buffer = fill_buffer(gated_rows(gates, whole_rows, tok_rows), target, experts, capacity)
    arrived = lax.all_to_all(buffer, "expert", split_axis=0, concat_axis=0, tiled=True)
    slot_rows = arrived.reshape(experts * capacity, whole_rows.shape[1])
    w_down = down_weight[0, 0]
    w_up = up_weight[0, 0]
    pre_slots = pre_act[0, 0].astype(jnp.float32)
    hidden = lax.dot_general(
        slot_rows, w_down, (((1,), (1,)), ((), ())), preferred_element_type=jnp.float32
    )
    pre_grad = (hidden * silu_slope(pre_slots)).astype(jnp.bfloat16)
    partial_value = lax.dot_general(
        pre_grad, w_up, (((1,), (1,)), ((), ())), preferred_element_type=jnp.float32
    )
    share = lax.psum_scatter(partial_value, "mp", scatter_dimension=1, tiled=True).astype(
        jnp.bfloat16
    )
    returned = lax.all_to_all(
        share.reshape(experts, capacity, share.shape[1]),
        "expert",
        split_axis=0,
        concat_axis=0,
        tiled=True,
    )
    picked = returned.reshape(experts * capacity, grad_rows.shape[1])[target]
    picked = picked.astype(jnp.float32).reshape(tok_rows, 2, grad_rows.shape[1])
    moe_total = grad_rows.astype(jnp.float32) + picked[:, 0, :] + picked[:, 1, :]
    grads_here = conv_grad[0]
    inputs_here = conv_input[0]
    taps = conv_weight[0]
    kernel_size = taps.shape[0]
    next_rows = shifted(grads_here[: kernel_size - 1], "expert", -1)
    prev_rows = shifted(inputs_here[tok_rows - kernel_size + 1 :], "expert", 1)
    grad_ext = jnp.concatenate([grads_here, next_rows], axis=0).astype(jnp.float32)
    input_ext = jnp.concatenate([prev_rows, inputs_here], axis=0).astype(jnp.float32)
    grad_local = grads_here.astype(jnp.float32)
    conv_result = jnp.zeros(grads_here.shape, jnp.float32)
    tap_terms = []
    for tap in range(kernel_size):
        start = kernel_size - 1 - tap
        conv_result = conv_result + taps[tap][None, :] * grad_ext[start : start + tok_rows]
        tap_terms.append(jnp.sum(grad_local * input_ext[tap : tap + tok_rows], axis=0))
    input_grad = conv_result.astype(jnp.bfloat16)
    tap_grads = lax.psum(jnp.stack(tap_terms), "expert")
    w_proj = in_proj[0]
    proj_partial = lax.dot_general(
        input_grad,
        lax.all_gather(w_proj, "expert", axis=0, tiled=True),
        (((1,), (1,)), ((), ())),
        preferred_element_type=jnp.float32,
    )
    proj_share = lax.psum_scatter(proj_partial, "mp", scatter_dimension=1, tiled=True)
    residual = (moe_total + proj_share).astype(jnp.bfloat16)
    sent_residual = shifted(residual, "section", -1)
    return (sent_residual[None], tap_grads[None])


def solution(mesh):
    in_specs = (
        P("section", "expert", "mp"),
        P("section", "expert", None),
        P("section", "expert", None),
        P("section", "expert", None, "mp"),
        P("section", "expert", "mp", None),
        P("section", "expert", None, "mp"),
        P("section", "expert", "mp"),
        P("section", "expert", "mp"),
        P("section", None, "mp"),
        P("section", "expert", "mp"),
    )
    out_specs = (P("section", "expert", "mp"), P("section", None, "mp"))
    return jax.shard_map(shards, mesh=mesh, in_specs=in_specs, out_specs=out_specs, check_vma=False)
```

profile of v0, /device:TPU:6, one launch (start us, length us, event | category | flops | bytes accessed | tf_op | source)
XLA Modules:
  0.0 510.5 jit_solution(10965666901345054638)
XLA Ops:
  12.7 15.3 %all-gather.5.cloned.1.call-done = bf16[1,128,4096]{2,1,0:T(8,128)(2,1)} async-done(((bf16[1,128,2048]{2,1,0:T(8,128)(2,1)}), bf16[1,128,4096]{2,1,0:T(8,128)(2,1)}) %all-gather.5.cloned.1.call-update) | async-done | bytes 1048592 | tf_op jit(solution)/shard_map/all_gather | solution.py:52
  27.9 1.4 bitcast_convert_fusion
  29.4 4.4 mul.101
  33.7 6.1 %mul.102 = f32[256,4096]{1,0:T(8,128)} reshape(f32[128,2,4096]{2,1,0:T(2,128)} %mul.101) | data formatting | bytes 8388608 | tf_op jit(solution)/shard_map/mul | solution.py:19
  39.8 7.7 %scatter_custom_fusion = bf16[512,4096]{1,0:T(8,128)(2,1)} fusion(s32[256]{0:T(256)S(1)} %bitcast.99, f32[256,4096]{1,0:T(8,128)} %mul.102, f32[256]{0:T(256)S(1)} %div.13, bf16[]{:T(256)} %constant.7.clone.1), kind=kCustom, calls=%fused_computation.9 | custom fusion | flops 2097152 | bytes 8389634 | tf_op jit(solution)/shard_map/scatter | solution.py:25
  47.5 106.0 %all_to_all.10 = bf16[32,16,4096]{2,1,0:T(8,128)(2,1)S(1)} all-to-all(bf16[32,16,4096]{2,1,0:T(8,128)(2,1)} %bitcast.85), channel_id=1, replica_groups=mesh['section'=4,'expert'=32,'mp'=2] {'expert'}, dimensions={0} | all-to-all | bytes 8388608 | tf_op jit(solution)/shard_map/all_to_all | solution.py:54
  153.6 2.5 fusion.12
  156.1 5.6 %fusion.2 = f32[512,4096]{1,0:T(8,128)} fusion(bf16[512,512]{1,0:T(8,128)(2,1)S(1)} %fusion.12, bf16[1,1,4096,512]{3,2,1,0:T(8,128)(2,1)S(1)} %copy-done), kind=kOutput, calls=%fused_computation.4 | convolution fusion | flops 2147483648 | bytes 13107200 | tf_op jit(solution)/shard_map/dot_general | solution.py:63
  162.8 1.3 collective-permute-start
  164.1 4.3 collective-permute-done
  168.5 12.6 %reduce-scatter.3.cloned.1.call-done = f32[512,2048]{1,0:T(8,128)} async-done(((f32[512,4096]{1,0:T(8,128)}), f32[512,2048]{1,0:T(8,128)}) %reduce-scatter.3.cloned.1.call-update) | async-done | bytes 4194320 | tf_op jit(solution)/shard_map/reduce_scatter | solution.py:66
  181.2 3.9 convert_element_type.68
  185.0 9.8 %all-to-all-start.1 = ((bf16[32,16,2048]{2,1,0:T(8,128)(2,1)}), bf16[32,16,2048]{2,1,0:T(8,128)(2,1)S(1)}, u32[]{:S(2)}, u32[]{:S(2)}) async-start(bf16[32,16,2048]{2,1,0:T(8,128)(2,1)} %bitcast.86), calls=%async_computation.2 | async-start | bytes 4194304 | tf_op jit(solution)/shard_map/all_to_all | solution.py:69
  194.9 133.4 %all-gather.7.cloned.1.call-done = bf16[1,4096,2048]{2,1,0:T(8,128)(2,1)} async-done(((bf16[1,128,2048]{2,1,0:T(8,128)(2,1)}), bf16[1,4096,2048]{2,1,0:T(8,128)(2,1)}) %all-gather.7.cloned.1.call-update) | async-done | bytes 16777232 | tf_op jit(solution)/shard_map/all_gather | solution.py:99
  328.3 12.8 %fusion = f32[128,4096]{1,0:T(8,128)} fusion(bf16[1,4096,2048]{2,1,0:T(8,128)(2,1)} %all-gather.7.cloned.1.call-done, f32[131,2048]{1,0:T(8,128)S(1)} %maximum_convert_fusion, f32[2048]{0:T(1024)S(1)} %bitcast.93, f32[2048]{0:T(1024)S(1)} %bitcast.94, f32[2048]{0:T(1024)S(1)} %bitcast.92, f32[2048]{0:T(1024)S(1)} %bitcast.91), kind=kOutput, calls=%fused_computation.2 | convolution fusion | flops 2149580800 | bytes 23101440 | tf_op jit(solution)/shard_map/dot_general | solution.py:97
  341.9 2.1 collective-permute-start.2
  344.0 1.4 gather_fusion
  345.4 1.3 reshape.97
  346.7 2.7 fusion.41
  349.4 4.0 reduce-scatter.5.cloned.1.call-done
  353.4 2.4 fusion.30
  355.8 2.8 collective-permute-start.1
  359.4 143.1 %psum.7 = f32[1,4,2048]{2,1,0:T(4,128)} all-reduce(f32[1,4,2048]{2,1,0:T(4,128)S(1)} %maximum_bitcast_fusion), channel_id=1, replica_groups=mesh['section'=4,'expert'=32,'mp'=2] {'expert'}, use_global_device_ids=true, to_apply=%region_10.11 | all-reduce | flops 8192 | bytes 65536 | tf_op jit(solution)/shard_map/psum | solution.py:95
  502.6 0.8 copy.36
  (49 shorter events, 7.4 us)
Async XLA Ops:
  8.0 19.9 %all-gather.5.cloned.1.call-start = ((), (), s32[]{:S(2)}) async-start(), calls=%async_computation.6 | async-start | bytes 1572864 | tf_op jit(solution)/shard_map/all_gather | solution.py:52
  8.7 172.4 %reduce-scatter.3.cloned.1.call-start = ((), (), s32[]{:S(2)}) async-start(), calls=%async_computation.4 | async-start | bytes 12582912 | tf_op jit(solution)/shard_map/reduce_scatter | solution.py:66
  47.5 106.0 %copy-start.5 = (bf16[1,1,512,4096]{3,2,1,0:T(8,128)(2,1)S(1)}, bf16[1,1,512,4096]{3,2,1,0:T(8,128)(2,1)}, u32[]{:S(2)}) copy-start(bf16[1,1,512,4096]{3,2,1,0:T(8,128)(2,1)} %param.14) | copy-start | bytes 12582916
  47.5 106.0 %copy-start.6 = (bf16[1,1,512,512]{3,2,1,0:T(8,128)(2,1)S(1)}, bf16[1,1,512,512]{3,2,1,0:T(8,128)(2,1)}, u32[]{:S(2)}) copy-start(bf16[1,1,512,512]{3,2,1,0:T(8,128)(2,1)} %param.15) | copy-start | bytes 1572868
  153.6 2.6 copy-start
  161.7 1.0 copy-start.1
  161.7 2.4 copy-start.4
  161.8 166.5 %all-gather.7.cloned.1.call-start = ((), (), s32[]{:S(2)}) async-start(), calls=%async_computation.7 | async-start | bytes 17301504 | tf_op jit(solution)/shard_map/all_gather | solution.py:99
  162.8 5.6 %collective-permute-start = (bf16[3,2048]{1,0:T(4,128)(2,1)S(1)}, bf16[3,2048]{1,0:T(4,128)(2,1)S(1)}, u32[]{:S(2)}, u32[]{:S(2)}) collective-permute-start(bf16[3,2048]{1,0:T(4,128)(2,1)S(1)} %slice_bitcast_fusion.1), channel_id=1, source_target_pairs={{2,0},{4,2},{6,4},{8,6},{10,8},{12,10},{14,12},{16,14},{18,16},{20... | collective-permute-start | bytes 36872 | tf_op jit(solution)/shard_map/ppermute | solution.py:10
  185.0 159.0 %all-to-all-start.1 = ((bf16[32,16,2048]{2,1,0:T(8,128)(2,1)}), bf16[32,16,2048]{2,1,0:T(8,128)(2,1)S(1)}, u32[]{:S(2)}, u32[]{:S(2)}) async-start(bf16[32,16,2048]{2,1,0:T(8,128)(2,1)} %bitcast.86), calls=%async_computation.2 | async-start | bytes 4194304 | tf_op jit(solution)/shard_map/all_to_all | solution.py:69
  194.8 158.6 %reduce-scatter.5.cloned.1.call-start = ((), (), s32[]{:S(2)}) async-start(), calls=%async_computation.5 | async-start | bytes 3145728 | tf_op jit(solution)/shard_map/reduce_scatter | solution.py:103
  341.9 16.7 %collective-permute-start.2 = (bf16[3,2048]{1,0:T(4,128)(2,1)S(1)}, bf16[3,2048]{1,0:T(4,128)(2,1)S(1)}, u32[]{:S(2)}, u32[]{:S(2)}) collective-permute-start(bf16[3,2048]{1,0:T(4,128)(2,1)S(1)} %slice_bitcast_fusion), channel_id=1, source_target_pairs={{0,2},{2,4},{4,6},{6,8},{8,10},{10,12},{12,14},{14,16},{16,18},{18... | collective-permute-start | bytes 36872 | tf_op jit(solution)/shard_map/ppermute | solution.py:10
  349.4 9.3 %copy-start.3 = (bf16[1,128,2048]{2,1,0:T(8,128)(2,1)S(1)}, bf16[1,128,2048]{2,1,0:T(8,128)(2,1)}, u32[]{:S(2)}) copy-start(bf16[1,128,2048]{2,1,0:T(8,128)(2,1)} %param.17) | copy-start | bytes 1572868
  349.4 9.4 %copy-start.2 = (bf16[1,128,2048]{2,1,0:T(8,128)(2,1)S(1)}, bf16[1,128,2048]{2,1,0:T(8,128)(2,1)}, u32[]{:S(2)}) copy-start(bf16[1,128,2048]{2,1,0:T(8,128)(2,1)} %param.16) | copy-start | bytes 1572868
  355.8 146.7 %collective-permute-start.1 = (bf16[128,2048]{1,0:T(8,128)(2,1)S(1)}, bf16[128,2048]{1,0:T(8,128)(2,1)S(1)}, u32[]{:S(2)}, u32[]{:S(2)}) collective-permute-start(bf16[128,2048]{1,0:T(8,128)(2,1)S(1)} %fusion.30), channel_id=1, source_target_pairs={{64,0},{128,64},{192,128},{65,1},{129,65},{193,129},{66,2},{130,66... | collective-permute-start | bytes 1572872 | tf_op jit(solution)/shard_map/ppermute | solution.py:10
Sparse Core Ops, SparseCore 0:
  10.6 17.2 all-gather.4
  161.9 19.2 reduce-scatter.2
  341.3 12.0 reduce-scatter.4
Sparse Core Ops, SparseCore 1:
  165.1 163.1 all-gather.6
where the time goes:
time: 511 us; the launch traced here: 510 us
  blocking collectives  249 us (49%)
  waiting for transfers between devices  171 us (33%)
  matrix products  21 us (4%)
  local copies, waits for them, and re-layouts  19.6 us (4%)
  other arithmetic  18.5 us (4%)
  starting transfers between devices  16.1 us (3%)
  between operations  15.4 us (3%)
    psum x1, blocking collectives, shards(): tap_grads = lax.psum(jnp.stack(tap_terms), 'expert')  143 us
    all_gather x1, waiting for transfers between devices, shards(): lax.all_gather(w_proj, 'expert', axis=0, tiled=True)  133 us
    all_to_all x1, blocking collectives, shards(): lax.all_to_all(buffer, 'expert', split_axis=0, concat_axis=0, tiled=True)  106 us
    all_gather x1, waiting for transfers between devices, shards(): whole_rows = lax.all_gather(grad_rows, 'mp', axis=1, tiled=True)  15.3 us
    dot_general x1, matrix products, shards(): lax.dot_general(input_grad, lax.all_gather(w_proj, 'expert', axis=0, tile...  12.8 us
    reduce_scatter x1, waiting for transfers between devices, shards(): lax.psum_scatter(partial_value, 'mp', scatter_dimension=1, tiled=True)  12.6 us
    mul x2, local copies, waits for them, and re-layouts, gated_rows(): gates[:, :, None] * rows.astype(jnp.float32)[:, None, :]  10.4 us
  transfers between devices with their start and end apart: 8, of which 5 were waited for; matrix products, arithmetic and copies ran while one was open for 6% of the time, Pallas kernels for 0%

commit v1 on v0

--- a/solution.py
+++ b/solution.py
@@ -92,7 +92,7 @@
         conv_result = conv_result + taps[tap][None, :] * grad_ext[start : start + tok_rows]
         tap_terms.append(jnp.sum(grad_local * input_ext[tap : tap + tok_rows], axis=0))
     input_grad = conv_result.astype(jnp.bfloat16)
-    tap_grads = lax.psum(jnp.stack(tap_terms), "expert")
+    tap_grads = jnp.sum(lax.all_gather(jnp.stack(tap_terms), "expert"), axis=0)
     w_proj = in_proj[0]
     proj_partial = lax.dot_general(
         input_grad,

time: 511 us -> 412 us (0.81)
  blocking collectives: 249 us -> 138 us
  waiting for transfers between devices: 171 us -> 180 us
    psum x1 -> x0, blocking collectives: 143 us -> none  [shards(): tap_grads = lax.psum(jnp.stack(tap_terms), 'expert')]
    all_gather x1, waiting for transfers between devices: 133 us -> 40 us  [shards(): lax.all_gather(w_proj, 'expert', axis=0, tiled=True)]
    all_gather x0 -> x1, waiting for transfers between devices: none -> 64.1 us  [shards(): tap_grads = jnp.sum(lax.all_gather(jnp.stack(tap_terms), 'expert'), axis=0)]
    all_to_all x1, waiting for transfers between devices: 0.01 us -> 43.5 us  [shards(): lax.all_to_all(share.reshape(experts, capacity, share.shape[1]), 'expert'...]
    all_to_all x1, blocking collectives: 106 us -> 138 us  [shards(): lax.all_to_all(buffer, 'expert', split_axis=0, concat_axis=0, tiled=True)]
  transfers between devices with their start and end apart: 8 -> 9, of which waited for: 5 -> 7; matrix products, arithmetic and copies ran while one was open for 6% -> 14% of each run, Pallas kernels for 0% -> 0%
where the time goes in v1:
time: 412 us; the launch traced here: 411 us
  waiting for transfers between devices  180 us (44%)
  blocking collectives  138 us (33%)
  other arithmetic  21 us (5%)
  matrix products  20.9 us (5%)
  local copies, waits for them, and re-layouts  19.3 us (5%)
  starting transfers between devices  18 us (4%)
  between operations  14 us (3%)
    all_to_all x1, blocking collectives, shards(): lax.all_to_all(buffer, 'expert', split_axis=0, concat_axis=0, tiled=True)  138 us
    all_gather x1, waiting for transfers between devices, shards(): tap_grads = jnp.sum(lax.all_gather(jnp.stack(tap_terms), 'expert'), axis=0)  64.1 us
    all_to_all x1, waiting for transfers between devices, shards(): lax.all_to_all(share.reshape(experts, capacity, share.shape[1]), 'expert'...  43.5 us
    all_gather x1, waiting for transfers between devices, shards(): lax.all_gather(w_proj, 'expert', axis=0, tiled=True)  40 us
    all_gather x1, waiting for transfers between devices, shards(): whole_rows = lax.all_gather(grad_rows, 'mp', axis=1, tiled=True)  14.5 us
    dot_general x1, matrix products, shards(): lax.dot_general(input_grad, lax.all_gather(w_proj, 'expert', axis=0, tile...  12.8 us
    mul x2, local copies, waits for them, and re-layouts, gated_rows(): gates[:, :, None] * rows.astype(jnp.float32)[:, None, :]  10.4 us
    reduce_scatter x1, waiting for transfers between devices, shards(): lax.psum_scatter(partial_value, 'mp', scatter_dimension=1, tiled=True)  10 us
  transfers between devices with their start and end apart: 9, of which 7 were waited for; matrix products, arithmetic and copies ran while one was open for 14% of the time, Pallas kernels for 0%

profile of v1, /device:TPU:6, one launch (start us, length us, event | category | flops | bytes accessed | tf_op | source)
XLA Modules:
  0.0 411.2 jit_solution(7926304286385347821)
XLA Ops:
  12.6 14.5 %all-gather.8.cloned.1.call-done = bf16[1,128,4096]{2,1,0:T(8,128)(2,1)} async-done(((bf16[1,128,2048]{2,1,0:T(8,128)(2,1)}), bf16[1,128,4096]{2,1,0:T(8,128)(2,1)}) %all-gather.8.cloned.1.call-update) | async-done | bytes 1048592 | tf_op jit(solution)/shard_map/all_gather | solution.py:52
  27.1 1.4 bitcast_convert_fusion
  28.6 4.3 %mul.101 = f32[128,2,4096]{2,1,0:T(2,128)} broadcast(f32[128,4096]{1,0:T(8,128)S(1)} %bitcast_convert_fusion), dimensions={0,2} | broadcast | bytes 6291456 | tf_op jit(solution)/shard_map/mul | solution.py:19
  32.9 6.1 %mul.102 = f32[256,4096]{1,0:T(8,128)} reshape(f32[128,2,4096]{2,1,0:T(2,128)} %mul.101) | data formatting | bytes 8388608 | tf_op jit(solution)/shard_map/mul | solution.py:19
  39.0 7.7 %scatter_custom_fusion = bf16[512,4096]{1,0:T(8,128)(2,1)} fusion(s32[256]{0:T(256)S(1)} %bitcast.101, f32[256,4096]{1,0:T(8,128)} %mul.102, f32[256]{0:T(256)S(1)} %div.13, bf16[]{:T(256)} %constant.7.clone.1), kind=kCustom, calls=%fused_computation.9 | custom fusion | flops 2097152 | bytes 8389634 | tf_op jit(solution)/shard_map/scatter | solution.py:25
  46.7 138.1 %all_to_all.10 = bf16[32,16,4096]{2,1,0:T(8,128)(2,1)S(1)} all-to-all(bf16[32,16,4096]{2,1,0:T(8,128)(2,1)} %bitcast.86), channel_id=1, replica_groups=mesh['section'=4,'expert'=32,'mp'=2] {'expert'}, dimensions={0} | all-to-all | bytes 8388608 | tf_op jit(solution)/shard_map/all_to_all | solution.py:54
  184.9 2.5 fusion.12
  187.4 5.6 %fusion.2 = f32[512,4096]{1,0:T(8,128)} fusion(bf16[512,512]{1,0:T(8,128)(2,1)S(1)} %fusion.12, bf16[1,1,4096,512]{3,2,1,0:T(8,128)(2,1)S(1)} %copy-done), kind=kOutput, calls=%fused_computation.4 | convolution fusion | flops 2147483648 | bytes 13107200 | tf_op jit(solution)/shard_map/dot_general | solution.py:63
  195.4 4.6 %collective-permute-done = bf16[3,2048]{1,0:T(4,128)(2,1)S(1)} collective-permute-done((bf16[3,2048]{1,0:T(4,128)(2,1)S(1)}, bf16[3,2048]{1,0:T(4,128)(2,1)S(1)}, u32[]{:S(2)}, u32[]{:S(2)}) %collective-permute-start) | collective-permute-done | bytes 12320 | tf_op jit(solution)/shard_map/ppermute | solution.py:10
  200.2 40.0 %all-gather.10.cloned.1.call-done = bf16[1,4096,2048]{2,1,0:T(8,128)(2,1)} async-done(((bf16[1,128,2048]{2,1,0:T(8,128)(2,1)}), bf16[1,4096,2048]{2,1,0:T(8,128)(2,1)}) %all-gather.10.cloned.1.call-update) | async-done | bytes 16777232 | tf_op jit(solution)/shard_map/all_gather | solution.py:99
  240.2 12.8 %fusion = f32[128,4096]{1,0:T(8,128)} fusion(bf16[1,4096,2048]{2,1,0:T(8,128)(2,1)} %all-gather.10.cloned.1.call-done, f32[131,2048]{1,0:T(8,128)S(1)} %maximum_convert_fusion, f32[2048]{0:T(1024)S(1)} %bitcast.94, f32[2048]{0:T(1024)S(1)} %bitcast.95, f32[2048]{0:T(1024)S(1)} %bitcast.93, f32[2048]{0:T(1024)S(1)} %bitcast.92), kind=kOutput, calls=%fused_computation.2 | convolution fusion | flops 2149580800 | bytes 23101440 | tf_op jit(solution)/shard_map/dot_general | solution.py:97
  253.0 10.0 %reduce-scatter.3.cloned.1.call-done = f32[512,2048]{1,0:T(8,128)} async-done(((f32[512,4096]{1,0:T(8,128)}), f32[512,2048]{1,0:T(8,128)}) %reduce-scatter.3.cloned.1.call-update) | async-done | bytes 4194320 | tf_op jit(solution)/shard_map/reduce_scatter | solution.py:66
  263.1 3.9 convert_element_type.68
  266.9 9.8 %all-to-all-start.1 = ((bf16[32,16,2048]{2,1,0:T(8,128)(2,1)}), bf16[32,16,2048]{2,1,0:T(8,128)(2,1)S(1)}, u32[]{:S(2)}, u32[]{:S(2)}) async-start(bf16[32,16,2048]{2,1,0:T(8,128)(2,1)} %bitcast.87), calls=%async_computation.2 | async-start | bytes 4194304 | tf_op jit(solution)/shard_map/all_to_all | solution.py:69
  276.8 3.9 collective-permute-start.2
  280.8 1.6 collective-permute-done.2
  283.8 43.5 %all-to-all-done.1 = bf16[32,16,2048]{2,1,0:T(8,128)(2,1)S(1)} async-done(((bf16[32,16,2048]{2,1,0:T(8,128)(2,1)}), bf16[32,16,2048]{2,1,0:T(8,128)(2,1)S(1)}, u32[]{:S(2)}, u32[]{:S(2)}) %all-to-all-start.1) | async-done | bytes 2097184 | tf_op jit(solution)/shard_map/all_to_all | solution.py:69
  327.3 1.4 gather_fusion
  328.7 1.3 reshape.97
  330.0 2.6 fusion.41
  332.6 2.4 fusion.30
  335.1 2.8 collective-permute-start.1
  337.9 64.1 %all-gather.12.cloned.1.call-done = f32[32,4,2048]{2,1,0:T(4,128)} async-done(((f32[1,4,2048]{2,1,0:T(4,128)}), f32[32,4,2048]{2,1,0:T(4,128)}) %all-gather.12.cloned.1.call-update) | async-done | bytes 1048592 | tf_op jit(solution)/shard_map/all_gather | solution.py:95
  401.9 2.0 reduce_sum.62
  (50 shorter events, 10.1 us)
Async XLA Ops:
  7.2 20.0 %all-gather.8.cloned.1.call-start = ((), (), s32[]{:S(2)}) async-start(), calls=%async_computation.6 | async-start | bytes 1572864 | tf_op jit(solution)/shard_map/all_gather | solution.py:52
  7.9 232.3 %all-gather.10.cloned.1.call-start = ((), (), s32[]{:S(2)}) async-start(), calls=%async_computation.7 | async-start | bytes 17301504 | tf_op jit(solution)/shard_map/all_gather | solution.py:99
  8.6 254.4 %reduce-scatter.3.cloned.1.call-start = ((), (), s32[]{:S(2)}) async-start(), calls=%async_computation.4 | async-start | bytes 12582912 | tf_op jit(solution)/shard_map/reduce_scatter | solution.py:66
  46.7 138.2 %copy-start.4 = (bf16[1,1,512,4096]{3,2,1,0:T(8,128)(2,1)S(1)}, bf16[1,1,512,4096]{3,2,1,0:T(8,128)(2,1)}, u32[]{:S(2)}) copy-start(bf16[1,1,512,4096]{3,2,1,0:T(8,128)(2,1)} %param.14) | copy-start | bytes 12582916
  46.7 138.2 %copy-start.5 = (bf16[1,1,512,512]{3,2,1,0:T(8,128)(2,1)S(1)}, bf16[1,1,512,512]{3,2,1,0:T(8,128)(2,1)}, u32[]{:S(2)}) copy-start(bf16[1,1,512,512]{3,2,1,0:T(8,128)(2,1)} %param.15) | copy-start | bytes 1572868
  184.9 2.6 copy-start
  193.0 1.1 copy-start.1
  193.0 2.4 copy-start.3
  193.0 139.6 %reduce-scatter.5.cloned.1.call-start = ((), (), s32[]{:S(2)}) async-start(), calls=%async_computation.5 | async-start | bytes 3145728 | tf_op jit(solution)/shard_map/reduce_scatter | solution.py:103
  194.1 6.0 %collective-permute-start = (bf16[3,2048]{1,0:T(4,128)(2,1)S(1)}, bf16[3,2048]{1,0:T(4,128)(2,1)S(1)}, u32[]{:S(2)}, u32[]{:S(2)}) collective-permute-start(bf16[3,2048]{1,0:T(4,128)(2,1)S(1)} %slice_bitcast_fusion.1), channel_id=1, source_target_pairs={{2,0},{4,2},{6,4},{8,6},{10,8},{12,10},{14,12},{16,14},{18,16},{20... | collective-permute-start | bytes 36872 | tf_op jit(solution)/shard_map/ppermute | solution.py:10
  253.0 23.8 %copy-start.2 = (bf16[1,128,2048]{2,1,0:T(8,128)(2,1)S(1)}, bf16[1,128,2048]{2,1,0:T(8,128)(2,1)}, u32[]{:S(2)}) copy-start(bf16[1,128,2048]{2,1,0:T(8,128)(2,1)} %param.17) | copy-start | bytes 1572868
  266.9 60.4 %all-to-all-start.1 = ((bf16[32,16,2048]{2,1,0:T(8,128)(2,1)}), bf16[32,16,2048]{2,1,0:T(8,128)(2,1)S(1)}, u32[]{:S(2)}, u32[]{:S(2)}) async-start(bf16[32,16,2048]{2,1,0:T(8,128)(2,1)} %bitcast.87), calls=%async_computation.2 | async-start | bytes 4194304 | tf_op jit(solution)/shard_map/all_to_all | solution.py:69
  276.8 125.2 %all-gather.12.cloned.1.call-start = ((), (), s32[]{:S(2)}) async-start(), calls=%async_computation.8 | async-start | bytes 1081344 | tf_op jit(solution)/shard_map/all_gather | solution.py:95
  276.8 5.6 %collective-permute-start.2 = (bf16[3,2048]{1,0:T(4,128)(2,1)S(1)}, bf16[3,2048]{1,0:T(4,128)(2,1)S(1)}, u32[]{:S(2)}, u32[]{:S(2)}) collective-permute-start(bf16[3,2048]{1,0:T(4,128)(2,1)S(1)} %slice_bitcast_fusion), channel_id=1, source_target_pairs={{0,2},{2,4},{4,6},{6,8},{8,10},{10,12},{12,14},{14,16},{16,18},{18... | collective-permute-start | bytes 36872 | tf_op jit(solution)/shard_map/ppermute | solution.py:10
  335.1 68.9 %collective-permute-start.1 = (bf16[128,2048]{1,0:T(8,128)(2,1)S(1)}, bf16[128,2048]{1,0:T(8,128)(2,1)S(1)}, u32[]{:S(2)}, u32[]{:S(2)}) collective-permute-start(bf16[128,2048]{1,0:T(8,128)(2,1)S(1)} %fusion.30), channel_id=1, source_target_pairs={{64,0},{128,64},{192,128},{65,1},{129,65},{193,129},{66,2},{130,66... | collective-permute-start | bytes 1572872 | tf_op jit(solution)/shard_map/ppermute | solution.py:10
Sparse Core Ops, SparseCore 0:
  9.8 17.2 all-gather.7
  29.7 210.4 all-gather.9
  242.7 20.2 reduce-scatter.2
  265.6 16.2 reduce-scatter.4
  284.8 117.0 all-gather.11
